TPU v7x, 32 devices: a whole 2x2x4 slice. The times are simulated.
32 devices in a mesh: dom: 8 (over z, core), grp: 4 (over y, x).
Axes of the slice: x: 2, y: 2, z: 4, core: 2. Of those that a mesh axis runs over, the one named last changes fastest.
Arguments:
- feats: bfloat16 [8192, 256], P(('dom', 'grp')), may hold values from -6 to 6
- w_self: bfloat16 [256, 256], replicated, may hold values from -0.375 to 0.375
- w_neigh: bfloat16 [256, 256], replicated, may hold values from -0.375 to 0.375
- local_tiles: bfloat16 [64, 3, 128, 128], P(('dom', 'grp')), may hold values from -0.15625 to 0.15625
- local_cols: int32 [64, 3], P(('dom', 'grp')), may hold values from 0 to 7, as said below
- cut_tiles: bfloat16 [64, 10, 128, 128], P(('dom', 'grp')), may hold values from -0.15625 to 0.15625
- cut_src: int32 [64, 10], P(('dom', 'grp')), may hold values from 0 to 7, as said below
- send_block: int32 [32, 8], P(('dom', 'grp')), may hold values from 0 to 1
- send_live: int32 [32, 8], P(('dom', 'grp')), may hold values from 0 to 1, as said below
- cotangent: bfloat16 [8192, 256], P(('dom', 'grp')), may hold values from -0.0625 to 0.0625
Outputs:
- layer_out: bfloat16 [8192, 256], P(('dom', 'grp'))
- grad_self: float32 [256, 256], replicated
- grad_neigh: float32 [256, 256], replicated
Inputs may be any that keep to these rules, and one draw needn't show every extreme that they name: `local_cols`: the 3 column blocks of one row block are distinct. `cut_src`: 0 marks an empty slot; the share of filled slots differs from partition to partition. send_live[e, p] is 1 exactly when some row block of device p * 4 + g (g the position of e) has a cut slot with offset naming e's partition; it is 0 where p is e's own partition.
All inputs are finite; a program needn't handle non-finite values.
Results may differ from a plain program's by a relative error of at most 0.0056.
Values may be sent and summed in bfloat16 or wider, within the bound.
A program may use at most 64 MiB of HBM per device.

v0:
```python
import jax
import jax.numpy as jnp
from jax import lax
from jax.sharding import PartitionSpec as P


def body(
    feats,
    w_self,
    w_neigh,
    local_tiles,
    local_cols,
    cut_tiles,
    cut_src,
    send_block,
    send_live,
    cotangent,
):
    row_blocks = local_tiles.shape[0]
    block_size = local_tiles.shape[2]
    features = feats.shape[1]
    partitions = lax.axis_size("dom")
    own_blocks = feats.reshape(row_blocks, block_size, features)
    gathered = lax.all_gather(feats, "grp", axis=0, tiled=True)
    picked = gathered.reshape(-1, block_size, features)[local_cols]
    aggregate_sum = jnp.einsum(
        "rkij,rkjf->rif", local_tiles, picked, preferred_element_type=jnp.float32
    )
    outgoing = own_blocks[send_block[0]] * send_live[0][:, None, None].astype(jnp.bfloat16)
    received = lax.all_to_all(outgoing, "dom", split_axis=0, concat_axis=0, tiled=True)
    source = (lax.axis_index("dom") + cut_src) % partitions
    remote = received[source]
    aggregate_sum = aggregate_sum + jnp.einsum(
        "rkij,rkjf->rif", cut_tiles, remote, preferred_element_type=jnp.float32
    )
    agg = aggregate_sum.reshape(row_blocks * block_size, features).astype(jnp.bfloat16)
    preact = jnp.dot(feats, w_self, preferred_element_type=jnp.float32) + jnp.dot(
        agg, w_neigh, preferred_element_type=jnp.float32
    )
    sigmoid = jax.nn.sigmoid(preact)
    layer_out = (preact * sigmoid).astype(jnp.bfloat16)
    grad_pre = (cotangent.astype(jnp.float32) * sigmoid * (1.0 + preact * (1.0 - sigmoid))).astype(
        jnp.bfloat16
    )
    grad_own = jnp.dot(feats.T, grad_pre, preferred_element_type=jnp.float32)
    grad_agg = jnp.dot(agg.T, grad_pre, preferred_element_type=jnp.float32)
    stacked = jnp.concatenate([grad_own, grad_agg], axis=0)
    shared = lax.psum_scatter(stacked, "grp", scatter_dimension=0, tiled=True)
    shared = lax.psum(shared, "dom")
    summed = lax.all_gather(shared, "grp", axis=0, tiled=True)
    return (layer_out, summed[:features], summed[features:])


def solution(mesh):
    return jax.shard_map(
        body,
        mesh=mesh,
        in_specs=(
            P(("dom", "grp"), None),
            P(),
            P(),
            P(("dom", "grp"), None, None, None),
            P(("dom", "grp"), None),
            P(("dom", "grp"), None, None, None),
            P(("dom", "grp"), None),
            P(("dom", "grp"), None),
            P(("dom", "grp"), None),
            P(("dom", "grp"), None),
        ),
        out_specs=(P(("dom", "grp"), None), P(), P()),
        check_vma=False,
    )
```

profile of v0, /device:TPU:0, one launch (start us, length us, event | category | flops | bytes accessed | tf_op | source)
XLA Modules:
  0.0 135.9 jit_solution(555693463951138174)
XLA Ops:
  7.2 0.7 fusion.3
  7.9 0.7 convert_bitcast_fusion
  8.6 1.5 %gather_fusion.1 = bf16[8,128,256]{2,1,0:T(8,128)(2,1)S(1)} fusion(bf16[2,128,256]{2,1,0:T(8,128)(2,1)} %bitcast.37, s32[1024]{0:T(1024)S(1)} %pad_clamp_fusion.1), kind=kCustom, calls=%fused_computation.1 | custom fusion | bytes 1048608 | tf_op jit(solution)/shard_map/gather | solution.py:29
  10.1 0.9 broadcast_multiply_fusion
  11.0 6.5 %all-to-all-start = ((bf16[8,128,256]{2,1,0:T(8,128)(2,1)}), bf16[8,128,256]{2,1,0:T(8,128)(2,1)S(1)}, u32[]{:S(2)}, u32[]{:S(2)}) async-start(bf16[8,128,256]{2,1,0:T(8,128)(2,1)} %broadcast_multiply_fusion), calls=%async_computation | async-start | bytes 1048576 | tf_op jit(solution)/shard_map/all_to_all | solution.py:30
  17.6 0.1 reshape.70
  17.6 0.1 reshape.54
  17.7 10.6 %all_gather.6 = bf16[1024,256]{1,0:T(8,128)(2,1)S(1)} all-gather(bf16[256,256]{1,0:T(8,128)(2,1)S(1)} %copy-done.1), channel_id=1, replica_groups=mesh['dom'=8,'grp'=4] {'grp'}, dimensions={0}, use_global_device_ids=true | all-gather | bytes 655360 | tf_op jit(solution)/shard_map/all_gather | solution.py:24
  28.3 0.6 gather_fusion
  28.9 0.2 convolution_bitcast_fusion
  29.2 0.2 fusion.5
  29.4 3.5 %all-to-all-done = bf16[8,128,256]{2,1,0:T(8,128)(2,1)S(1)} async-done(((bf16[8,128,256]{2,1,0:T(8,128)(2,1)}), bf16[8,128,256]{2,1,0:T(8,128)(2,1)S(1)}, u32[]{:S(2)}, u32[]{:S(2)}) %all-to-all-start) | async-done | bytes 524320 | tf_op jit(solution)/shard_map/all_to_all | solution.py:30
  32.8 0.6 gather_fusion.2
  33.5 0.3 fusion.1
  33.9 0.5 copy-done.6
  34.4 0.1 copy-done.7
  34.4 0.9 multiply_convert_fusion
  35.4 0.2 fusion.6
  35.6 0.2 convolution_bitcast_fusion.1
  35.8 0.8 pad_maximum_fusion
  36.8 23.8 %reduce-scatter.2.cloned.1.call-done = f32[128,256]{1,0:T(8,128)} async-done(((f32[512,256]{1,0:T(8,128)}), f32[128,256]{1,0:T(8,128)}) %reduce-scatter.2.cloned.1.call-update) | async-done | bytes 131088 | tf_op jit(solution)/shard_map/reduce_scatter | solution.py:48
  60.6 56.7 %all-reduce.2.cloned.1.call-done = f32[128,256]{1,0:T(8,128)} async-done(((f32[128,256]{1,0:T(8,128)}), f32[128,256]{1,0:T(8,128)}) %all-reduce.2.cloned.1.call-update) | async-done | bytes 131088 | tf_op jit(solution)/shard_map/psum | solution.py:49
  117.2 11.0 %all_gather.7 = f32[512,256]{1,0:T(8,128)S(1)} all-gather(f32[128,256]{1,0:T(8,128)} %all-reduce.2.cloned.1.call-done), channel_id=1, replica_groups=mesh['dom'=8,'grp'=4] {'grp'}, dimensions={0}, use_global_device_ids=true | all-gather | bytes 655360 | tf_op jit(solution)/shard_map/all_gather | solution.py:50
  128.3 0.8 fusion.4
  (23 shorter events, 0.2 us)
Async XLA Ops:
  7.2 26.3 %copy-start = (bf16[2,10,128,128]{3,2,1,0:T(8,128)(2,1)S(1)}, bf16[2,10,128,128]{3,2,1,0:T(8,128)(2,1)}, u32[]{:S(2)}) copy-start(bf16[2,10,128,128]{3,2,1,0:T(8,128)(2,1)} %param.15) | copy-start | bytes 1966084
  10.1 7.5 %copy-start.4 = (s32[2,10]{1,0:T(2,128)S(1)}, s32[2,10]{1,0:T(2,128)}, u32[]{:S(2)}) copy-start(s32[2,10]{1,0:T(2,128)} %param.16) | copy-start | bytes 244
  10.1 7.6 %copy-start.5 = (s32[2,3]{1,0:T(2,128)S(1)}, s32[2,3]{1,0:T(2,128)}, u32[]{:S(2)}) copy-start(s32[2,3]{1,0:T(2,128)} %param.14) | copy-start | bytes 76
  10.1 7.6 %copy-start.1 = (bf16[256,256]{1,0:T(8,128)(2,1)S(1)}, bf16[256,256]{1,0:T(8,128)(2,1)}, u32[]{:S(2)}) copy-start(bf16[256,256]{1,0:T(8,128)(2,1)} %param.10) | copy-start | bytes 393220
  11.0 17.9 %copy-start.2 = (bf16[2,3,128,128]{3,2,1,0:T(8,128)(2,1)S(1)}, bf16[2,3,128,128]{3,2,1,0:T(8,128)(2,1)}, u32[]{:S(2)}) copy-start(bf16[2,3,128,128]{3,2,1,0:T(8,128)(2,1)} %param.13) | copy-start | bytes 589828
  11.0 21.8 %all-to-all-start = ((bf16[8,128,256]{2,1,0:T(8,128)(2,1)}), bf16[8,128,256]{2,1,0:T(8,128)(2,1)S(1)}, u32[]{:S(2)}, u32[]{:S(2)}) async-start(bf16[8,128,256]{2,1,0:T(8,128)(2,1)} %broadcast_multiply_fusion), calls=%async_computation | async-start | bytes 1048576 | tf_op jit(solution)/shard_map/all_to_all | solution.py:30
  17.5 11.7 %copy-start.3 = (bf16[256,256]{1,0:T(8,128)(2,1)S(1)}, bf16[256,256]{1,0:T(8,128)(2,1)}, u32[]{:S(2)}) copy-start(bf16[256,256]{1,0:T(8,128)(2,1)} %param.11) | copy-start | bytes 393220
  17.5 43.1 %reduce-scatter.2.cloned.1.call-start = ((), (), s32[]{:S(2)}) async-start(), calls=%async_computation.2 | async-start | bytes 655360 | tf_op jit(solution)/shard_map/reduce_scatter | solution.py:48
  33.5 0.9 copy-start.6
  33.5 1.0 copy-start.7
  36.7 80.5 %all-reduce.2.cloned.1.call-start = ((), (), s32[]{:S(2)}) async-start(), calls=%async_computation.3 | async-start | bytes 262144 | tf_op jit(solution)/shard_map/psum | solution.py:49
Sparse Core Ops, SparseCore 0:
  36.8 23.6 reduce-scatter.1
  63.0 54.2 all-reduce.1
where the time goes:
time: 136 us
  waiting for transfers between devices  84 us (62%)
  blocking collectives  21.6 us (16%)
  between operations  14.2 us (10%)
  starting transfers between devices  6.54 us (5%)
  local copies, waits for them, and re-layouts  4.3 us (3%)
  other arithmetic  3.17 us (2%)
  matrix products  2.14 us (2%)
    psum x1, waiting for transfers between devices, body(): shared = lax.psum(shared, 'dom')  56.7 us
    reduce_scatter x1, waiting for transfers between devices, body(): shared = lax.psum_scatter(stacked, 'grp', scatter_dimension=0, tiled=True)  23.8 us
    all_gather x1, blocking collectives, body(): summed = lax.all_gather(shared, 'grp', axis=0, tiled=True)  11 us
    all_gather x1, blocking collectives, body(): gathered = lax.all_gather(feats, 'grp', axis=0, tiled=True)  10.6 us
    all_to_all x1, starting transfers between devices, body(): lax.all_to_all(outgoing, 'dom', split_axis=0, concat_axis=0, tiled=True)  6.46 us
    all_to_all x1, waiting for transfers between devices, body(): lax.all_to_all(outgoing, 'dom', split_axis=0, concat_axis=0, tiled=True)  3.46 us
  transfers between devices with their start and end apart: 3, of which 3 were waited for; matrix products, arithmetic and copies ran while one was open for 1% of the time, Pallas kernels for 0%

commit v1 on v0

v1 whole, which is shorter than its diff:
```python
import functools

import jax
import jax.numpy as jnp
from jax import lax
from jax.experimental import pallas as pl
from jax.experimental.pallas import tpu as pltpu
from jax.sharding import PartitionSpec as P

MESH = pl.DeviceIdType.MESH
PACK = 16


def f32_dot(a, b):
    return jnp.dot(a, b, preferred_element_type=jnp.float32)


def kernel(
    n_dom,
    n_grp,
    cols_ref,
    src_ref,
    block_ref,
    live_ref,
    feats_ref,
    w_self_ref,
    w_neigh_ref,
    local_ref,
    cut_ref,
    cot_ref,
    out_ref,
    grad_ref,
    near,
    outgoing,
    far,
    acc,
    part,
    part_low,
    sums1,
    mid,
    sums2,
    near_send,
    near_recv,
    far_send,
    far_recv,
    s1_send,
    s1_recv,
    s2_send,
    s2_recv,
    s3_send,
    s3_recv,
    s4_send,
    s4_recv,
):
    row_blocks, local_slots, block, _ = local_ref.shape
    cut_slots = cut_ref.shape[1]
    features = feats_ref.shape[2]
    me_d, me_g = lax.axis_index("dom"), lax.axis_index("grp")
    dom_peer = [lax.rem(me_d + o, n_dom) for o in range(n_dom)]
    grp_peer = [lax.rem(me_g + o, n_grp) for o in range(n_grp)]

    def remote(src, dst, send, recv, o, axis):
        peer = dom_peer[o] if axis == "dom" else grp_peer[o]
        return pltpu.make_async_remote_copy(
            src_ref=src,
            dst_ref=dst,
            send_sem=send.at[o],
            recv_sem=recv.at[o],
            device_id={axis: peer},
            device_id_type=MESH,
        )

    barrier = pltpu.get_barrier_semaphore()
    for o in range(1, n_dom):
        pl.semaphore_signal(barrier, inc=1, device_id={"dom": dom_peer[o]}, device_id_type=MESH)
    for o in range(1, n_grp):
        pl.semaphore_signal(barrier, inc=1, device_id={"grp": grp_peer[o]}, device_id_type=MESH)

    for o in range(n_dom):
        alive = live_ref[0, dom_peer[o]].astype(jnp.float32)
        chosen = feats_ref[block_ref[0, dom_peer[o]]].astype(jnp.float32)
        target = far if o == 0 else outgoing
        target[o] = (chosen * alive).astype(jnp.bfloat16)
    pl.semaphore_wait(barrier, n_dom + n_grp - 2)

    far_copies = [
        remote(outgoing.at[o], far.at[o], far_send, far_recv, o, "dom") for o in range(1, n_dom)
    ]
    near_copies = [
        remote(
            feats_ref,
            near.at[pl.ds(o * row_blocks, row_blocks)],
            near_send,
            near_recv,
            o,
            "grp",
        )
        for o in range(1, n_grp)
    ]
    for copy in far_copies + near_copies:
        copy.start()

    near[0:row_blocks] = feats_ref[...]
    for copy in near_copies:
        copy.wait()
    for b in range(row_blocks):
        total = jnp.zeros((block, features), jnp.float32)
        for k in range(local_slots):
            col = cols_ref[b, k]
            owner = lax.div(col, row_blocks)
            slot = lax.rem(me_g - owner + n_grp, n_grp)
            where = slot * row_blocks + lax.rem(col, row_blocks)
            total = total + f32_dot(local_ref[b, k], near[where])
        acc[b] = total

    for copy in far_copies:
        copy.wait()
    grads_own = jnp.zeros((features, features), jnp.float32)
    grads_agg = jnp.zeros((features, features), jnp.float32)
    for b in range(row_blocks):
        total = acc[b]
        for k in range(cut_slots):
            slot = lax.rem(n_dom - src_ref[b, k], n_dom)
            total = total + f32_dot(cut_ref[b, k], far[slot])
        agg = total.astype(jnp.bfloat16)
        own = feats_ref[b]
        preact = f32_dot(own, w_self_ref[...]) + f32_dot(agg, w_neigh_ref[...])
        sig = jax.nn.sigmoid(preact)
        out_ref[b] = (preact * sig).astype(jnp.bfloat16)
        grad_pre = (
            cot_ref[b].astype(jnp.float32) * sig * (1.0 + preact * (1.0 - sig))
        ).astype(jnp.bfloat16)
        dims = (((0,), (0,)), ((), ()))
        grads_own = grads_own + lax.dot_general(
            own, grad_pre, dims, preferred_element_type=jnp.float32
        )
        grads_agg = grads_agg + lax.dot_general(
            agg, grad_pre, dims, preferred_element_type=jnp.float32
        )
    part[0:features] = grads_own
    part[features : 2 * features] = grads_agg
    part_low[0:features] = grads_own.astype(jnp.bfloat16)
    part_low[features : 2 * features] = grads_agg.astype(jnp.bfloat16)

    rows = 2 * features // n_grp
    mine = pl.ds(pl.multiple_of(me_g * rows, rows), rows)
    copies = [
        remote(
            part_low.at[pl.ds(pl.multiple_of(grp_peer[o] * rows, rows), rows)],
            sums1.at[o],
            s1_send,
            s1_recv,
            o,
            "grp",
        )
        for o in range(1, n_grp)
    ]
    for copy in copies:
        copy.start()
    total = part[mine]
    for o, copy in enumerate(copies, 1):
        copy.wait()
        total = total + sums1[o].astype(jnp.float32)
    mid[...] = total

    if rows % (PACK * n_dom) == 0:
        piece = rows // n_dom
        here = pl.ds(pl.multiple_of(me_d * piece, piece), piece)
        copies = [
            remote(
                mid.at[pl.ds(pl.multiple_of(dom_peer[o] * piece, piece), piece)],
                sums2.at[o],
                s2_send,
                s2_recv,
                o,
                "dom",
            )
            for o in range(1, n_dom)
        ]
        for copy in copies:
            copy.start()
        total = mid[here]
        for o, copy in enumerate(copies, 1):
            copy.wait()
            total = total + sums2[o]
        spot = pl.ds(pl.multiple_of(me_g * rows + me_d * piece, piece), piece)
        grad_ref[spot] = total.astype(jnp.bfloat16)
        copies = [
            remote(grad_ref.at[spot], grad_ref.at[spot], s3_send, s3_recv, o, "dom")
            for o in range(1, n_dom)
        ]
        for copy in copies:
            copy.start()
        for copy in copies:
            copy.wait()
    else:
        copies = [
            remote(mid, sums2.at[o], s2_send, s2_recv, o, "dom") for o in range(1, n_dom)
        ]
        for copy in copies:
            copy.start()
        total = mid[...]
        for o, copy in enumerate(copies, 1):
            copy.wait()
            total = total + sums2[o]
        grad_ref[mine] = total.astype(jnp.bfloat16)

    copies = [
        remote(grad_ref.at[mine], grad_ref.at[mine], s4_send, s4_recv, o, "grp")
        for o in range(1, n_grp)
    ]
    for copy in copies:
        copy.start()
    for copy in copies:
        copy.wait()


def body(
    feats,
    w_self,
    w_neigh,
    local_tiles,
    local_cols,
    cut_tiles,
    cut_src,
    send_block,
    send_live,
    cotangent,
):
    row_blocks, _, block, _ = local_tiles.shape
    features = feats.shape[1]
    n_dom, n_grp = lax.axis_size("dom"), lax.axis_size("grp")
    blocks = (row_blocks, block, features)
    rows = 2 * features // n_grp
    piece = rows // n_dom if rows % (PACK * n_dom) == 0 else rows
    dma = pltpu.SemaphoreType.DMA
    smem = pl.BlockSpec(memory_space=pltpu.SMEM)
    vmem = pl.BlockSpec(memory_space=pltpu.VMEM)
    out, grads = pl.pallas_call(
        functools.partial(kernel, n_dom, n_grp),
        out_shape=(
            jax.ShapeDtypeStruct(blocks, jnp.bfloat16),
            jax.ShapeDtypeStruct((2 * features, features), jnp.bfloat16),
        ),
        in_specs=[smem] * 4 + [vmem] * 6,
        out_specs=(vmem, vmem),
        scratch_shapes=[
            pltpu.VMEM((n_grp * row_blocks, block, features), jnp.bfloat16),
            pltpu.VMEM((n_dom, block, features), jnp.bfloat16),
            pltpu.VMEM((n_dom, block, features), jnp.bfloat16),
            pltpu.VMEM(blocks, jnp.float32),
            pltpu.VMEM((2 * features, features), jnp.float32),
            pltpu.VMEM((2 * features, features), jnp.bfloat16),
            pltpu.VMEM((n_grp, rows, features), jnp.bfloat16),
            pltpu.VMEM((rows, features), jnp.float32),
            pltpu.VMEM((n_dom, piece, features), jnp.float32),
        ]
        + [dma((n_grp,))] * 2
        + [dma((n_dom,))] * 2
        + [dma((n_grp,))] * 2
        + [dma((n_dom,))] * 4
        + [dma((n_grp,))] * 2,
        compiler_params=pltpu.CompilerParams(
            collective_id=0, has_side_effects=True, vmem_limit_bytes=32 * 2**20
        ),
    )(
        local_cols,
        cut_src,
        send_block,
        send_live,
        feats.reshape(blocks),
        w_self,
        w_neigh,
        local_tiles,
        cut_tiles,
        cotangent.reshape(blocks),
    )
    summed = grads.astype(jnp.float32)
    return (out.reshape(feats.shape), summed[:features], summed[features:])


def solution(mesh):
    return jax.shard_map(
        body,
        mesh=mesh,
        in_specs=(
            P(("dom", "grp"), None),
            P(),
            P(),
            P(("dom", "grp"), None, None, None),
            P(("dom", "grp"), None),
            P(("dom", "grp"), None, None, None),
            P(("dom", "grp"), None),
            P(("dom", "grp"), None),
            P(("dom", "grp"), None),
            P(("dom", "grp"), None),
        ),
        out_specs=(P(("dom", "grp"), None), P(), P()),
        check_vma=False,
    )
```

time: 136 us -> 47.1 us (0.35)
  waiting for transfers between devices: 84 us -> 0 us
  Pallas kernels: 0 us -> 38.3 us
  blocking collectives: 21.6 us -> 0 us
  between operations: 14.2 us -> 0.68 us
  starting transfers between devices: 6.54 us -> 0 us
  local copies, waits for them, and re-layouts: 4.3 us -> 7.79 us
  other arithmetic: 3.17 us -> 0 us
  matrix products: 2.14 us -> 0 us
    psum x1 -> x0, waiting for transfers between devices: 56.7 us -> none  [body(): shared = lax.psum(shared, 'dom')]
    pallas_call x0 -> x1, Pallas kernels: none -> 38.3 us  [body(): pl.pallas_call(functools.partial(kernel, n_dom, n_grp), out_shape=(jax.Sh...]
    reduce_scatter x1 -> x0, waiting for transfers between devices: 23.8 us -> none  [body(): shared = lax.psum_scatter(stacked, 'grp', scatter_dimension=0, tiled=True)]
    all_gather x2 -> x0, blocking collectives: 21.6 us -> none  [the longest x1 11 us: body(): summed = lax.all_gather(shared, 'grp', axis=0, tiled=True)]
    all_to_all x1 -> x0, starting transfers between devices: 6.46 us -> none  [body(): lax.all_to_all(outgoing, 'dom', split_axis=0, concat_axis=0, tiled=True)]
    unnamed x16 -> x21, local copies, waits for them, and re-layouts: 0.63 us -> 6.96 us
    all_to_all x1 -> x0, waiting for transfers between devices: 3.46 us -> none  [body(): lax.all_to_all(outgoing, 'dom', split_axis=0, concat_axis=0, tiled=True)]
    gather x3 -> x0, local copies, waits for them, and re-layouts: 2.68 us -> none  [the longest x1 1.48 us: body(): own_blocks[send_block[0]] * send_live[0][:, None, None].astype(jnp.bfloat16)]
  transfers between devices with their start and end apart: 3 -> 0, of which waited for: 3 -> 0; matrix products, arithmetic and copies ran while one was open for 1% -> 0% of each run, Pallas kernels for 0% -> 0%
where the time goes in v1:
time: 47.1 us; the launch traced here: 46.8 us
  Pallas kernels  38.3 us (81%)
  local copies, waits for them, and re-layouts  7.79 us (17%)
  between operations  0.68 us (1%)
    pallas_call x1, Pallas kernels, body(): pl.pallas_call(functools.partial(kernel, n_dom, n_grp), out_shape=(jax.Sh...  38.3 us
    unnamed x21, local copies, waits for them, and re-layouts  6.96 us

profile of v1, /device:TPU:0, one launch (start us, length us, event | category | flops | bytes accessed | tf_op | source)
XLA Modules:
  0.0 46.8 jit_solution(4838509606760807671)
XLA Ops:
  0.6 0.0 copy-start.7
  0.6 0.0 copy-start.9
  0.7 0.0 copy-start.6
  0.7 0.0 copy-start.8
  0.7 0.6 %copy-done.7 = s32[2,10]{1,0:T(2,128)S(1)} copy-done((s32[2,10]{1,0:T(2,128)S(1)}, s32[2,10]{1,0:T(2,128)}, u32[]{:S(2)}) %copy-start.7) | copy-done | bytes 104
  1.3 0.0 copy-done.9
  1.3 0.0 copy-done.6
  1.3 0.0 copy-done.8
  1.3 0.0 copy-start
  1.4 1.1 %copy-done = bf16[2,10,128,128]{3,2,1,0:T(8,128)(2,1)S(1)} copy-done((bf16[2,10,128,128]{3,2,1,0:T(8,128)(2,1)S(1)}, bf16[2,10,128,128]{3,2,1,0:T(8,128)(2,1)}, u32[]{:S(2)}) %copy-start) | copy-done | bytes 655384
  2.4 0.0 copy-start.1
  2.4 0.9 %copy-done.1 = bf16[2,3,128,128]{3,2,1,0:T(8,128)(2,1)S(1)} copy-done((bf16[2,3,128,128]{3,2,1,0:T(8,128)(2,1)S(1)}, bf16[2,3,128,128]{3,2,1,0:T(8,128)(2,1)}, u32[]{:S(2)}) %copy-start.1) | copy-done | bytes 196632
  3.4 0.0 copy-start.2
  3.4 0.9 %copy-done.2 = bf16[256,256]{1,0:T(8,128)(2,1)S(1)} copy-done((bf16[256,256]{1,0:T(8,128)(2,1)S(1)}, bf16[256,256]{1,0:T(8,128)(2,1)}, u32[]{:S(2)}) %copy-start.2) | copy-done | bytes 131096
  4.3 0.0 copy-start.3
  4.3 0.9 %copy-done.3 = bf16[256,256]{1,0:T(8,128)(2,1)S(1)} copy-done((bf16[256,256]{1,0:T(8,128)(2,1)S(1)}, bf16[256,256]{1,0:T(8,128)(2,1)}, u32[]{:S(2)}) %copy-start.3) | copy-done | bytes 131096
  5.2 0.0 copy-start.4
  5.2 0.9 %copy-done.4 = bf16[256,256]{1,0:T(8,128)(2,1)S(1)} copy-done((bf16[256,256]{1,0:T(8,128)(2,1)S(1)}, bf16[256,256]{1,0:T(8,128)(2,1)}, u32[]{:S(2)}) %copy-start.4) | copy-done | bytes 131096
  6.1 0.0 copy-start.5
  6.1 0.9 %copy-done.5 = bf16[256,256]{1,0:T(8,128)(2,1)S(1)} copy-done((bf16[256,256]{1,0:T(8,128)(2,1)S(1)}, bf16[256,256]{1,0:T(8,128)(2,1)}, u32[]{:S(2)}) %copy-start.5) | copy-done | bytes 131096
  7.0 38.3 %shard_map.121 = (bf16[2,128,256]{2,1,0:T(8,128)(2,1)S(1)}, bf16[512,256]{1,0:T(8,128)(2,1)S(1)}) custom-call(s32[2,3]{1,0:T(2,128)S(1)} %copy-done.6, s32[2,10]{1,0:T(2,128)S(1)} %copy-done.7, s32[1,8]{1,0:T(1,128)S(1)} %copy-done.8, s32[1,8]{1,0:T(1,128)S(1)} %copy-done.9, bf16[2,128,256]{2,1,0:T(8,128)(2,1)S(1)} %bitcast.3, ...), custom_call_target="tpu_custom_call" | custom-call | tf_op jit(solution)/shard_map/pallas_call | solution.py:239
  45.3 0.8 %fusion = (f32[256,256]{1,0:T(8,128)}, f32[256,256]{1,0:T(8,128)}) fusion(bf16[512,256]{1,0:T(8,128)(2,1)S(1)} %get-tuple-element.6), kind=kLoop, calls=%fused_computation | loop fusion | bytes 1048576 | tf_op jit(solution)/shard_map/slice | solution.py:279
  46.1 0.7 %copy.14 = bf16[256,256]{1,0:T(8,128)(2,1)} copy(bf16[256,256]{1,0:T(8,128)(2,1)S(1)} %bitcast.5) | data formatting | bytes 262144
Async XLA Ops:
  0.6 0.7 %copy-start.7 = (s32[2,10]{1,0:T(2,128)S(1)}, s32[2,10]{1,0:T(2,128)}, u32[]{:S(2)}) copy-start(s32[2,10]{1,0:T(2,128)} %src_ref.1) | copy-start | bytes 244
  0.6 0.7 %copy-start.9 = (s32[1,8]{1,0:T(1,128)S(1)}, s32[1,8]{1,0:T(1,128)}, u32[]{:S(2)}) copy-start(s32[1,8]{1,0:T(1,128)} %live_ref.1) | copy-start | bytes 100
  0.7 0.7 %copy-start.6 = (s32[2,3]{1,0:T(2,128)S(1)}, s32[2,3]{1,0:T(2,128)}, u32[]{:S(2)}) copy-start(s32[2,3]{1,0:T(2,128)} %cols_ref.1) | copy-start | bytes 76
  0.7 0.7 %copy-start.8 = (s32[1,8]{1,0:T(1,128)S(1)}, s32[1,8]{1,0:T(1,128)}, u32[]{:S(2)}) copy-start(s32[1,8]{1,0:T(1,128)} %block_ref.1) | copy-start | bytes 100
  1.3 1.1 %copy-start = (bf16[2,10,128,128]{3,2,1,0:T(8,128)(2,1)S(1)}, bf16[2,10,128,128]{3,2,1,0:T(8,128)(2,1)}, u32[]{:S(2)}) copy-start(bf16[2,10,128,128]{3,2,1,0:T(8,128)(2,1)} %cut_ref.1) | copy-start | bytes 1966084
  2.4 0.9 %copy-start.1 = (bf16[2,3,128,128]{3,2,1,0:T(8,128)(2,1)S(1)}, bf16[2,3,128,128]{3,2,1,0:T(8,128)(2,1)}, u32[]{:S(2)}) copy-start(bf16[2,3,128,128]{3,2,1,0:T(8,128)(2,1)} %local_ref.1) | copy-start | bytes 589828
  3.4 0.9 %copy-start.2 = (bf16[256,256]{1,0:T(8,128)(2,1)S(1)}, bf16[256,256]{1,0:T(8,128)(2,1)}, u32[]{:S(2)}) copy-start(bf16[256,256]{1,0:T(8,128)(2,1)} %param.10) | copy-start | bytes 393220
  4.3 0.9 %copy-start.3 = (bf16[256,256]{1,0:T(8,128)(2,1)S(1)}, bf16[256,256]{1,0:T(8,128)(2,1)}, u32[]{:S(2)}) copy-start(bf16[256,256]{1,0:T(8,128)(2,1)} %w_self_ref.1) | copy-start | bytes 393220
  5.2 0.9 %copy-start.4 = (bf16[256,256]{1,0:T(8,128)(2,1)S(1)}, bf16[256,256]{1,0:T(8,128)(2,1)}, u32[]{:S(2)}) copy-start(bf16[256,256]{1,0:T(8,128)(2,1)} %w_neigh_ref.1) | copy-start | bytes 393220
  6.1 0.9 %copy-start.5 = (bf16[256,256]{1,0:T(8,128)(2,1)S(1)}, bf16[256,256]{1,0:T(8,128)(2,1)}, u32[]{:S(2)}) copy-start(bf16[256,256]{1,0:T(8,128)(2,1)} %param.19) | copy-start | bytes 393220

commit v2 on v1

v2 whole, which is shorter than its diff:
```python
import functools

import jax
import jax.numpy as jnp
from jax import lax
from jax.experimental import pallas as pl
from jax.experimental.pallas import tpu as pltpu
from jax.sharding import PartitionSpec as P

MESH = pl.DeviceIdType.MESH
PACK = 16


def f32_dot(a, b):
    return jnp.dot(a, b, preferred_element_type=jnp.float32)


def kernel(
    n_dom,
    n_grp,
    cols_hbm,
    src_hbm,
    block_hbm,
    live_hbm,
    feats_hbm,
    w_self_hbm,
    w_neigh_hbm,
    local_hbm,
    cut_hbm,
    cot_hbm,
    out_ref,
    grad_ref,
    cols_ref,
    src_ref,
    block_ref,
    live_ref,
    w_self_ref,
    w_neigh_ref,
    local_ref,
    cut_ref,
    cot_ref,
    feats_ref,
    near,
    outgoing,
    far,
    acc,
    pre,
    part,
    part_low,
    sums1,
    mid,
    sums2,
    load_sem,
    near_send,
    near_recv,
    far_send,
    far_recv,
    s1_send,
    s1_recv,
    s2_send,
    s2_recv,
    s3_send,
    s3_recv,
    s4_send,
    s4_recv,
):
    row_blocks, local_slots, block, _ = local_ref.shape
    cut_slots = cut_ref.shape[1]
    features = w_self_ref.shape[0]
    halves, _, width = part.shape
    me_d, me_g = lax.axis_index("dom"), lax.axis_index("grp")
    dom_peer = [lax.rem(me_d + o, n_dom) for o in range(n_dom)]
    grp_peer = [lax.rem(me_g + o, n_grp) for o in range(n_grp)]

    def remote(src, dst, send, recv, o, axis):
        peer = dom_peer[o] if axis == "dom" else grp_peer[o]
        return pltpu.make_async_remote_copy(
            src_ref=src,
            dst_ref=dst,
            send_sem=send,
            recv_sem=recv,
            device_id={axis: peer},
            device_id_type=MESH,
        )

    def begin(copies):
        for copy in copies:
            copy.start()
        return copies

    loads = begin(
        [
            pltpu.make_async_copy(src, dst, load_sem.at[i])
            for i, (src, dst) in enumerate(
                (
                    (block_hbm, block_ref),
                    (live_hbm, live_ref),
                    (feats_hbm, feats_ref),
                    (feats_hbm, near.at[pl.ds(0, row_blocks)]),
                    (cols_hbm, cols_ref),
                    (src_hbm, src_ref),
                    (w_self_hbm, w_self_ref),
                    (local_hbm, local_ref),
                    (cut_hbm, cut_ref),
                    (w_neigh_hbm, w_neigh_ref),
                    (cot_hbm, cot_ref),
                )
            )
        ]
    )
    barrier = pltpu.get_barrier_semaphore()
    for o in range(1, n_dom):
        pl.semaphore_signal(barrier, inc=1, device_id={"dom": dom_peer[o]}, device_id_type=MESH)
    for o in range(1, n_grp):
        pl.semaphore_signal(barrier, inc=1, device_id={"grp": grp_peer[o]}, device_id_type=MESH)
    for load in loads[:3]:
        load.wait()

    for o in range(n_dom):
        alive = live_ref[0, dom_peer[o]].astype(jnp.float32)
        chosen = feats_ref[block_ref[0, dom_peer[o]]].astype(jnp.float32)
        target = far if o == 0 else outgoing
        target[o] = (chosen * alive).astype(jnp.bfloat16)
    pl.semaphore_wait(barrier, n_dom + n_grp - 2)

    far_copies = begin(
        [
            remote(outgoing.at[o], far.at[o], far_send.at[o], far_recv.at[o], o, "dom")
            for o in range(1, n_dom)
        ]
    )
    near_copies = begin(
        [
            remote(
                feats_ref,
                near.at[pl.ds(o * row_blocks, row_blocks)],
                near_send.at[o],
                near_recv.at[o],
                o,
                "grp",
            )
            for o in range(1, n_grp)
        ]
    )

    for load in loads[3:]:
        load.wait()
    for b in range(row_blocks):
        pre[b] = f32_dot(feats_ref[b], w_self_ref[...])
    for copy in near_copies:
        copy.wait()
    for b in range(row_blocks):
        total = jnp.zeros((block, features), jnp.float32)
        for k in range(local_slots):
            col = cols_ref[b, k]
            owner = lax.div(col, row_blocks)
            slot = lax.rem(me_g - owner + n_grp, n_grp)
            where = slot * row_blocks + lax.rem(col, row_blocks)
            total = total + f32_dot(local_ref[b, k], near[where])
        acc[b] = total

    for copy in far_copies:
        copy.wait()
    grads_own = jnp.zeros((features, features), jnp.float32)
    grads_agg = jnp.zeros((features, features), jnp.float32)
    for b in range(row_blocks):
        total = acc[b]
        for k in range(cut_slots):
            slot = lax.rem(n_dom - src_ref[b, k], n_dom)
            total = total + f32_dot(cut_ref[b, k], far[slot])
        agg = total.astype(jnp.bfloat16)
        own = feats_ref[b]
        preact = pre[b] + f32_dot(agg, w_neigh_ref[...])
        sig = jax.nn.sigmoid(preact)
        out_ref[b] = (preact * sig).astype(jnp.bfloat16)
        grad_pre = (
            cot_ref[b].astype(jnp.float32) * sig * (1.0 + preact * (1.0 - sig))
        ).astype(jnp.bfloat16)
        dims = (((0,), (0,)), ((), ()))
        grads_own = grads_own + lax.dot_general(
            own, grad_pre, dims, preferred_element_type=jnp.float32
        )
        grads_agg = grads_agg + lax.dot_general(
            agg, grad_pre, dims, preferred_element_type=jnp.float32
        )

    rows = 2 * features // n_grp
    mine = pl.ds(pl.multiple_of(me_g * rows, rows), rows)
    split = rows % (PACK * n_dom) == 0
    piece = rows // n_dom if split else rows
    here = pl.ds(pl.multiple_of(me_d * piece, piece), piece) if split else pl.ds(0, rows)
    spot = (
        pl.ds(pl.multiple_of(me_g * rows + me_d * piece, piece), piece) if split else mine
    )

    columns = [pl.ds(h * width, width) for h in range(halves)]

    first = []
    for h in range(halves):
        cut = slice(h * width, (h + 1) * width)
        part[h, 0:features] = grads_own[:, cut]
        part[h, features : 2 * features] = grads_agg[:, cut]
        part_low[h, 0:features] = grads_own[:, cut].astype(jnp.bfloat16)
        part_low[h, features : 2 * features] = grads_agg[:, cut].astype(jnp.bfloat16)
        first.append(
            begin(
                [
                    remote(
                        part_low.at[h, pl.ds(pl.multiple_of(grp_peer[o] * rows, rows), rows)],
                        sums1.at[h, o],
                        s1_send.at[h, o],
                        s1_recv.at[h, o],
                        o,
                        "grp",
                    )
                    for o in range(1, n_grp)
                ]
            )
        )
    second = []
    for h in range(halves):
        total = part[h, mine]
        for o, copy in enumerate(first[h], 1):
            copy.wait()
            total = total + sums1[h, o].astype(jnp.float32)
        mid[h] = total
        second.append(
            begin(
                [
                    remote(
                        mid.at[
                            h,
                            pl.ds(pl.multiple_of(dom_peer[o] * piece, piece), piece)
                            if split
                            else pl.ds(0, rows),
                        ],
                        sums2.at[h, o],
                        s2_send.at[h, o],
                        s2_recv.at[h, o],
                        o,
                        "dom",
                    )
                    for o in range(1, n_dom)
                ]
            )
        )
    third = []
    for h in range(halves):
        total = mid[h, here]
        for o, copy in enumerate(second[h], 1):
            copy.wait()
            total = total + sums2[h, o]
        grad_ref[spot, columns[h]] = total.astype(jnp.bfloat16)
        if split:
            third.append(
                begin(
                    [
                        remote(
                            grad_ref.at[spot, columns[h]],
                            grad_ref.at[spot, columns[h]],
                            s3_send.at[h, o],
                            s3_recv.at[h, o],
                            o,
                            "dom",
                        )
                        for o in range(1, n_dom)
                    ]
                )
            )
    fourth = []
    for h in range(halves):
        if split:
            for copy in third[h]:
                copy.wait()
        fourth += begin(
            [
                remote(
                    grad_ref.at[mine, columns[h]],
                    grad_ref.at[mine, columns[h]],
                    s4_send.at[h, o],
                    s4_recv.at[h, o],
                    o,
                    "grp",
                )
                for o in range(1, n_grp)
            ]
        )
    for copy in fourth:
        copy.wait()


def body(
    feats,
    w_self,
    w_neigh,
    local_tiles,
    local_cols,
    cut_tiles,
    cut_src,
    send_block,
    send_live,
    cotangent,
):
    row_blocks, _, block, _ = local_tiles.shape
    features = feats.shape[1]
    n_dom, n_grp = lax.axis_size("dom"), lax.axis_size("grp")
    blocks = (row_blocks, block, features)
    rows = 2 * features // n_grp
    piece = rows // n_dom if rows % (PACK * n_dom) == 0 else rows
    halves = 2
    width = features // halves
    dma = pltpu.SemaphoreType.DMA
    hbm = pl.BlockSpec(memory_space=pltpu.HBM)
    vmem = pl.BlockSpec(memory_space=pltpu.VMEM)
    out, grads = pl.pallas_call(
        functools.partial(kernel, n_dom, n_grp),
        out_shape=(
            jax.ShapeDtypeStruct(blocks, jnp.bfloat16),
            jax.ShapeDtypeStruct((2 * features, features), jnp.bfloat16),
        ),
        in_specs=[hbm] * 10,
        out_specs=(vmem, vmem),
        scratch_shapes=[
            pltpu.SMEM(local_cols.shape, jnp.int32),
            pltpu.SMEM(cut_src.shape, jnp.int32),
            pltpu.SMEM(send_block.shape, jnp.int32),
            pltpu.SMEM(send_live.shape, jnp.int32),
            pltpu.VMEM(w_self.shape, jnp.bfloat16),
            pltpu.VMEM(w_neigh.shape, jnp.bfloat16),
            pltpu.VMEM(local_tiles.shape, jnp.bfloat16),
            pltpu.VMEM(cut_tiles.shape, jnp.bfloat16),
            pltpu.VMEM(blocks, jnp.bfloat16),
            pltpu.VMEM(blocks, jnp.bfloat16),
            pltpu.VMEM((n_grp * row_blocks, block, features), jnp.bfloat16),
            pltpu.VMEM((n_dom, block, features), jnp.bfloat16),
            pltpu.VMEM((n_dom, block, features), jnp.bfloat16),
            pltpu.VMEM(blocks, jnp.float32),
            pltpu.VMEM(blocks, jnp.float32),
            pltpu.VMEM((halves, 2 * features, width), jnp.float32),
            pltpu.VMEM((halves, 2 * features, width), jnp.bfloat16),
            pltpu.VMEM((halves, n_grp, rows, width), jnp.bfloat16),
            pltpu.VMEM((halves, rows, width), jnp.float32),
            pltpu.VMEM((halves, n_dom, piece, width), jnp.float32),
            dma((11,)),
        ]
        + [dma((n_grp,))] * 2
        + [dma((n_dom,))] * 2
        + [dma((halves, n_grp))] * 2
        + [dma((halves, n_dom))] * 4
        + [dma((halves, n_grp))] * 2,
        compiler_params=pltpu.CompilerParams(
            collective_id=0, has_side_effects=True, vmem_limit_bytes=60 * 2**20
        ),
    )(
        local_cols,
        cut_src,
        send_block,
        send_live,
        feats.reshape(blocks),
        w_self,
        w_neigh,
        local_tiles,
        cut_tiles,
        cotangent.reshape(blocks),
    )
    summed = grads.astype(jnp.float32)
    return (out.reshape(feats.shape), summed[:features], summed[features:])


def solution(mesh):
    return jax.shard_map(
        body,
        mesh=mesh,
        in_specs=(
            P(("dom", "grp"), None),
            P(),
            P(),
            P(("dom", "grp"), None, None, None),
            P(("dom", "grp"), None),
            P(("dom", "grp"), None, None, None),
            P(("dom", "grp"), None),
            P(("dom", "grp"), None),
            P(("dom", "grp"), None),
            P(("dom", "grp"), None),
        ),
        out_specs=(P(("dom", "grp"), None), P(), P()),
        check_vma=False,
    )
```

time: 47.1 us -> 39.9 us (0.85)
  local copies, waits for them, and re-layouts: 7.79 us -> 2.49 us
  Pallas kernels: 38.3 us -> 36.6 us
    unnamed x21 -> x3, local copies, waits for them, and re-layouts: 6.96 us -> 0.66 us
    pallas_call x1, Pallas kernels: 38.3 us -> 36.6 us  [body(): pl.pallas_call(functools.partial(kernel, n_dom, n_grp), out_shape=(jax.Sh...]
    slice x1, local copies, waits for them, and re-layouts: 0.83 us -> 1.83 us  [body(): return (out.reshape(feats.shape), summed[:features], summed[features:])]
where the time goes in v2:
time: 39.9 us; the launch traced here: 39.7 us
  Pallas kernels  36.6 us (92%)
  local copies, waits for them, and re-layouts  2.49 us (6%)
  between operations  0.65 us (2%)
    pallas_call x1, Pallas kernels, body(): pl.pallas_call(functools.partial(kernel, n_dom, n_grp), out_shape=(jax.Sh...  36.6 us
    slice x1, local copies, waits for them, and re-layouts, body(): return (out.reshape(feats.shape), summed[:features], summed[features:])  1.83 us

profile of v2, /device:TPU:0, one launch (start us, length us, event | category | flops | bytes accessed | tf_op | source)
XLA Modules:
  0.0 39.7 jit_solution(16084571620019432516)
XLA Ops:
  0.6 36.6 %shard_map.121 = (bf16[2,128,256]{2,1,0:T(8,128)(2,1)}, bf16[512,256]{1,0:T(8,128)(2,1)}) custom-call(s32[2,3]{1,0:T(2,128)} %cols_hbm.1, s32[2,10]{1,0:T(2,128)} %src_hbm.1, s32[1,8]{1,0:T(1,128)} %block_hbm.1, s32[1,8]{1,0:T(1,128)} %live_hbm.1, bf16[2,128,256]{2,1,0:T(8,128)(2,1)} %bitcast.3, bf16[256,256]{1,0:T(8,128)(2,1)} %w_self_hbm.1, ...), custom_call_target="tpu_custom_call" | custom-call | tf_op jit(solution)/shard_map/pallas_call | solution.py:315
  37.2 0.0 copy-start
  37.2 1.8 %fusion = (f32[256,256]{1,0:T(8,128)}, f32[256,256]{1,0:T(8,128)}) fusion(bf16[512,256]{1,0:T(8,128)(2,1)} %get-tuple-element.6), kind=kLoop, calls=%fused_computation | loop fusion | bytes 1048576 | tf_op jit(solution)/shard_map/slice | solution.py:367
  39.1 0.0 copy-done
  39.1 0.7 %copy.14 = bf16[256,256]{1,0:T(8,128)(2,1)} copy(bf16[256,256]{1,0:T(8,128)(2,1)S(1)} %bitcast.5) | data formatting | bytes 262144
Async XLA Ops:
  37.2 1.8 %copy-start = (bf16[2,128,256]{2,1,0:T(8,128)(2,1)S(1)}, bf16[2,128,256]{2,1,0:T(8,128)(2,1)}, u32[]{:S(2)}) copy-start(bf16[2,128,256]{2,1,0:T(8,128)(2,1)} %get-tuple-element.5) | copy-start | bytes 393220

commit v3 on v2

--- a/solution.py
+++ b/solution.py
@@ -9,6 +9,11 @@
 
 MESH = pl.DeviceIdType.MESH
 PACK = 16
+ORDERS = (("grp", "dom"), ("dom", "grp"))
+
+
+def piece_rows(rows, n):
+    return rows // n if rows % (PACK * n) == 0 else rows
 
 
 def f32_dot(a, b):
@@ -47,9 +52,14 @@
     pre,
     part,
     part_low,
-    sums1,
-    mid,
-    sums2,
+    sums1_a,
+    sums1_b,
+    mid_a,
+    mid_b,
+    low_a,
+    low_b,
+    sums2_a,
+    sums2_b,
     load_sem,
     near_send,
     near_recv,
@@ -64,10 +74,12 @@
     s4_send,
     s4_recv,
 ):
+    sums1, mid, mid_low = (sums1_a, sums1_b), (mid_a, mid_b), (low_a, low_b)
+    sums2 = (sums2_a, sums2_b)
     row_blocks, local_slots, block, _ = local_ref.shape
     cut_slots = cut_ref.shape[1]
     features = w_self_ref.shape[0]
-    halves, _, width = part.shape
+    width = part.shape[2]
     me_d, me_g = lax.axis_index("dom"), lax.axis_index("grp")
     dom_peer = [lax.rem(me_d + o, n_dom) for o in range(n_dom)]
     grp_peer = [lax.rem(me_g + o, n_grp) for o in range(n_grp)]
@@ -184,106 +196,110 @@
             agg, grad_pre, dims, preferred_element_type=jnp.float32
         )
 
-    rows = 2 * features // n_grp
-    mine = pl.ds(pl.multiple_of(me_g * rows, rows), rows)
-    split = rows % (PACK * n_dom) == 0
-    piece = rows // n_dom if split else rows
-    here = pl.ds(pl.multiple_of(me_d * piece, piece), piece) if split else pl.ds(0, rows)
-    spot = (
-        pl.ds(pl.multiple_of(me_g * rows + me_d * piece, piece), piece) if split else mine
-    )
-
-    columns = [pl.ds(h * width, width) for h in range(halves)]
+    peers = {"grp": grp_peer, "dom": dom_peer}
+    here = {"grp": me_g, "dom": me_d}
+    count = {"grp": n_grp, "dom": n_dom}
+
+    def rows_at(start, size):
+        return pl.ds(pl.multiple_of(start, size), size)
+
+    def to_peers(axis, src, dst, send, recv):
+        return begin(
+            [
+                remote(src(o), dst(o), send.at[o], recv.at[o], o, axis)
+                for o in range(1, count[axis])
+            ]
+        )
+
+    flows = []
+    for h, (one, two) in enumerate(ORDERS):
+        rows = 2 * features // count[one]
+        piece = piece_rows(rows, count[two])
+        split = piece < rows
+        flows.append(
+            dict(
+                one=one,
+                two=two,
+                rows=rows,
+                piece=piece,
+                split=split,
+                columns=pl.ds(h * width, width),
+                mine=rows_at(here[one] * rows, rows),
+                inner=rows_at(here[two] * piece, piece) if split else pl.ds(0, rows),
+                spot=rows_at(here[one] * rows + (here[two] * piece if split else 0), piece),
+                sums1=sums1[h],
+                mid=mid[h],
+                mid_low=mid_low[h],
+                sums2=sums2[h],
+            )
+        )
 
     first = []
-    for h in range(halves):
+    for h, f in enumerate(flows):
         cut = slice(h * width, (h + 1) * width)
         part[h, 0:features] = grads_own[:, cut]
         part[h, features : 2 * features] = grads_agg[:, cut]
         part_low[h, 0:features] = grads_own[:, cut].astype(jnp.bfloat16)
         part_low[h, features : 2 * features] = grads_agg[:, cut].astype(jnp.bfloat16)
         first.append(
-            begin(
-                [
-                    remote(
-                        part_low.at[h, pl.ds(pl.multiple_of(grp_peer[o] * rows, rows), rows)],
-                        sums1.at[h, o],
-                        s1_send.at[h, o],
-                        s1_recv.at[h, o],
-                        o,
-                        "grp",
-                    )
-                    for o in range(1, n_grp)
-                ]
+            to_peers(
+                f["one"],
+                lambda o: part_low.at[h, rows_at(peers[f["one"]][o] * f["rows"], f["rows"])],
+                lambda o: f["sums1"].at[o],
+                s1_send.at[h],
+                s1_recv.at[h],
             )
         )
     second = []
-    for h in range(halves):
-        total = part[h, mine]
+    for h, f in enumerate(flows):
+        total = part[h, f["mine"]]
         for o, copy in enumerate(first[h], 1):
             copy.wait()
-            total = total + sums1[h, o].astype(jnp.float32)
-        mid[h] = total
+            total = total + f["sums1"][o].astype(jnp.float32)
+        f["mid"][...] = total
+        f["mid_low"][...] = total.astype(jnp.bfloat16)
         second.append(
-            begin(
-                [
-                    remote(
-                        mid.at[
-                            h,
-                            pl.ds(pl.multiple_of(dom_peer[o] * piece, piece), piece)
-                            if split
-                            else pl.ds(0, rows),
-                        ],
-                        sums2.at[h, o],
-                        s2_send.at[h, o],
-                        s2_recv.at[h, o],
-                        o,
-                        "dom",
-                    )
-                    for o in range(1, n_dom)
-                ]
+            to_peers(
+                f["two"],
+                lambda o: f["mid_low"].at[rows_at(peers[f["two"]][o] * f["piece"], f["piece"])]
+                if f["split"]
+                else f["mid_low"],
+                lambda o: f["sums2"].at[o],
+                s2_send.at[h],
+                s2_recv.at[h],
             )
         )
     third = []
-    for h in range(halves):
-        total = mid[h, here]
+    for h, f in enumerate(flows):
+        total = f["mid"][f["inner"]]
         for o, copy in enumerate(second[h], 1):
             copy.wait()
-            total = total + sums2[h, o]
-        grad_ref[spot, columns[h]] = total.astype(jnp.bfloat16)
-        if split:
+            total = total + f["sums2"][o].astype(jnp.float32)
+        grad_ref[f["spot"], f["columns"]] = total.astype(jnp.bfloat16)
+        if f["split"]:
+            block_of = grad_ref.at[f["spot"], f["columns"]]
             third.append(
-                begin(
-                    [
-                        remote(
-                            grad_ref.at[spot, columns[h]],
-                            grad_ref.at[spot, columns[h]],
-                            s3_send.at[h, o],
-                            s3_recv.at[h, o],
-                            o,
-                            "dom",
-                        )
-                        for o in range(1, n_dom)
-                    ]
+                to_peers(
+                    f["two"],
+                    lambda o: block_of,
+                    lambda o: block_of,
+                    s3_send.at[h],
+                    s3_recv.at[h],
                 )
             )
+        else:
+            third.append([])
     fourth = []
-    for h in range(halves):
-        if split:
-            for copy in third[h]:
-                copy.wait()
-        fourth += begin(
-            [
-                remote(
-                    grad_ref.at[mine, columns[h]],
-                    grad_ref.at[mine, columns[h]],
-                    s4_send.at[h, o],
-                    s4_recv.at[h, o],
-                    o,
-                    "grp",
-                )
-                for o in range(1, n_grp)
-            ]
+    for h, f in enumerate(flows):
+        for copy in third[h]:
+            copy.wait()
+        rows_of = grad_ref.at[f["mine"], f["columns"]]
+        fourth += to_peers(
+            f["one"],
+            lambda o: rows_of,
+            lambda o: rows_of,
+            s4_send.at[h],
+            s4_recv.at[h],
         )
     for copy in fourth:
         copy.wait()
@@ -305,9 +321,13 @@
     features = feats.shape[1]
     n_dom, n_grp = lax.axis_size("dom"), lax.axis_size("grp")
     blocks = (row_blocks, block, features)
-    rows = 2 * features // n_grp
-    piece = rows // n_dom if rows % (PACK * n_dom) == 0 else rows
-    halves = 2
+    halves = len(ORDERS)
+    count = {"grp": n_grp, "dom": n_dom}
+    most = max(n_grp, n_dom)
+    sizes = []
+    for one, two in ORDERS:
+        rows = 2 * features // count[one]
+        sizes.append((count[one], rows, count[two], piece_rows(rows, count[two])))
     width = features // halves
     dma = pltpu.SemaphoreType.DMA
     hbm = pl.BlockSpec(memory_space=pltpu.HBM)
@@ -338,16 +358,17 @@
             pltpu.VMEM(blocks, jnp.float32),
             pltpu.VMEM((halves, 2 * features, width), jnp.float32),
             pltpu.VMEM((halves, 2 * features, width), jnp.bfloat16),
-            pltpu.VMEM((halves, n_grp, rows, width), jnp.bfloat16),
-            pltpu.VMEM((halves, rows, width), jnp.float32),
-            pltpu.VMEM((halves, n_dom, piece, width), jnp.float32),
+        ]
+        + [pltpu.VMEM((n, r, width), jnp.bfloat16) for n, r, _, _ in sizes]
+        + [pltpu.VMEM((r, width), jnp.float32) for _, r, _, _ in sizes]
+        + [pltpu.VMEM((r, width), jnp.bfloat16) for _, r, _, _ in sizes]
+        + [pltpu.VMEM((n, p, width), jnp.bfloat16) for _, _, n, p in sizes]
+        + [
             dma((11,)),
         ]
         + [dma((n_grp,))] * 2
         + [dma((n_dom,))] * 2
-        + [dma((halves, n_grp))] * 2
-        + [dma((halves, n_dom))] * 4
-        + [dma((halves, n_grp))] * 2,
+        + [dma((halves, most))] * 8,
         compiler_params=pltpu.CompilerParams(
             collective_id=0, has_side_effects=True, vmem_limit_bytes=60 * 2**20
         ),

time: 39.9 us -> 39.6 us (level)
  no operation moved by 1% of the time
where the time goes in v3:
time: 39.6 us; the launch traced here: 39.5 us
  Pallas kernels  36.3 us (92%)
  local copies, waits for them, and re-layouts  2.49 us (6%)
  between operations  0.65 us (2%)
    pallas_call x1, Pallas kernels, body(): pl.pallas_call(functools.partial(kernel, n_dom, n_grp), out_shape=(jax.Sh...  36.3 us
    slice x1, local copies, waits for them, and re-layouts, body(): return (out.reshape(feats.shape), summed[:features], summed[features:])  1.83 us

profile of v3, /device:TPU:0, one launch (start us, length us, event | category | flops | bytes accessed | tf_op | source)
XLA Modules:
  0.0 39.5 jit_solution(6955665699929477076)
XLA Ops:
  0.6 36.3 %shard_map.121 = (bf16[2,128,256]{2,1,0:T(8,128)(2,1)}, bf16[512,256]{1,0:T(8,128)(2,1)}) custom-call(s32[2,3]{1,0:T(2,128)} %cols_hbm.1, s32[2,10]{1,0:T(2,128)} %src_hbm.1, s32[1,8]{1,0:T(1,128)} %block_hbm.1, s32[1,8]{1,0:T(1,128)} %live_hbm.1, bf16[2,128,256]{2,1,0:T(8,128)(2,1)} %bitcast.3, bf16[256,256]{1,0:T(8,128)(2,1)} %w_self_hbm.1, ...), custom_call_target="tpu_custom_call" | custom-call | tf_op jit(solution)/shard_map/pallas_call | solution.py:335
  37.0 0.0 copy-start
  37.0 1.8 %fusion = (f32[256,256]{1,0:T(8,128)}, f32[256,256]{1,0:T(8,128)}) fusion(bf16[512,256]{1,0:T(8,128)(2,1)} %get-tuple-element.6), kind=kLoop, calls=%fused_computation | loop fusion | bytes 1048576 | tf_op jit(solution)/shard_map/slice | solution.py:388
  38.8 0.0 copy-done
  38.8 0.7 %copy.14 = bf16[256,256]{1,0:T(8,128)(2,1)} copy(bf16[256,256]{1,0:T(8,128)(2,1)S(1)} %bitcast.5) | data formatting | bytes 262144
Async XLA Ops:
  37.0 1.8 %copy-start = (bf16[2,128,256]{2,1,0:T(8,128)(2,1)S(1)}, bf16[2,128,256]{2,1,0:T(8,128)(2,1)}, u32[]{:S(2)}) copy-start(bf16[2,128,256]{2,1,0:T(8,128)(2,1)} %get-tuple-element.5) | copy-start | bytes 393220

commit v4 on v3

--- a/solution.py
+++ b/solution.py
@@ -160,7 +160,7 @@
     for b in range(row_blocks):
         pre[b] = f32_dot(feats_ref[b], w_self_ref[...])
     for copy in near_copies:
-        copy.wait()
+        copy.wait_recv()
     for b in range(row_blocks):
         total = jnp.zeros((block, features), jnp.float32)
         for k in range(local_slots):
@@ -172,7 +172,7 @@
         acc[b] = total
 
     for copy in far_copies:
-        copy.wait()
+        copy.wait_recv()
     grads_own = jnp.zeros((features, features), jnp.float32)
     grads_agg = jnp.zeros((features, features), jnp.float32)
     for b in range(row_blocks):
@@ -254,7 +254,7 @@
     for h, f in enumerate(flows):
         total = part[h, f["mine"]]
         for o, copy in enumerate(first[h], 1):
-            copy.wait()
+            copy.wait_recv()
             total = total + f["sums1"][o].astype(jnp.float32)
         f["mid"][...] = total
         f["mid_low"][...] = total.astype(jnp.bfloat16)
@@ -273,7 +273,7 @@
     for h, f in enumerate(flows):
         total = f["mid"][f["inner"]]
         for o, copy in enumerate(second[h], 1):
-            copy.wait()
+            copy.wait_recv()
             total = total + f["sums2"][o].astype(jnp.float32)
         grad_ref[f["spot"], f["columns"]] = total.astype(jnp.bfloat16)
         if f["split"]:
@@ -292,7 +292,7 @@
     fourth = []
     for h, f in enumerate(flows):
         for copy in third[h]:
-            copy.wait()
+            copy.wait_recv()
         rows_of = grad_ref.at[f["mine"], f["columns"]]
         fourth += to_peers(
             f["one"],
@@ -302,7 +302,11 @@
             s4_recv.at[h],
         )
     for copy in fourth:
-        copy.wait()
+        copy.wait_recv()
+
+    sent = [far_copies, near_copies, *first, *second, *third, fourth]
+    for copy in [copy for group in sent for copy in group]:
+        copy.wait_send()
 
 
 def body(
@@ -370,19 +374,24 @@
         + [dma((n_dom,))] * 2
         + [dma((halves, most))] * 8,
         compiler_params=pltpu.CompilerParams(
-            collective_id=0, has_side_effects=True, vmem_limit_bytes=60 * 2**20
+            collective_id=0, has_side_effects=True, vmem_limit_bytes=32 * 2**20
         ),
     )(
-        local_cols,
-        cut_src,
-        send_block,
-        send_live,
-        feats.reshape(blocks),
-        w_self,
-        w_neigh,
-        local_tiles,
-        cut_tiles,
-        cotangent.reshape(blocks),
+        *(
+            pltpu.with_memory_space_constraint(x, pltpu.HBM)
+            for x in (
+                local_cols,
+                cut_src,
+                send_block,
+                send_live,
+                feats.reshape(blocks),
+                w_self,
+                w_neigh,
+                local_tiles,
+                cut_tiles,
+                cotangent.reshape(blocks),
+            )
+        )
     )
     summed = grads.astype(jnp.float32)
     return (out.reshape(feats.shape), summed[:features], summed[features:])

time: 39.6 us -> 37.9 us (0.957)
  local copies, waits for them, and re-layouts: 2.49 us -> 1.48 us
  Pallas kernels: 36.3 us -> 35.6 us
    slice x1, local copies, waits for them, and re-layouts: 1.83 us -> 0.83 us  [body(): return (out.reshape(feats.shape), summed[:features], summed[features:])]
    pallas_call x1, Pallas kernels: 36.3 us -> 35.6 us  [body(): pl.pallas_call(functools.partial(kernel, n_dom, n_grp), out_shape=(jax.Sh...]
where the time goes in v4:
time: 37.9 us; the launch traced here: 37.7 us
  Pallas kernels  35.6 us (94%)
  local copies, waits for them, and re-layouts  1.48 us (4%)
  between operations  0.64 us (2%)
    pallas_call x1, Pallas kernels, body(): pl.pallas_call(functools.partial(kernel, n_dom, n_grp), out_shape=(jax.Sh...  35.6 us
    slice x1, local copies, waits for them, and re-layouts, body(): return (out.reshape(feats.shape), summed[:features], summed[features:])  0.83 us

profile of v4, /device:TPU:0, one launch (start us, length us, event | category | flops | bytes accessed | tf_op | source)
XLA Modules:
  0.0 37.7 jit_solution(271301757797403989)
XLA Ops:
  0.6 35.6 %shard_map.121 = (bf16[2,128,256]{2,1,0:T(8,128)(2,1)S(1)}, bf16[512,256]{1,0:T(8,128)(2,1)S(1)}) custom-call(s32[2,3]{1,0:T(2,128)} %cols_hbm.1, s32[2,10]{1,0:T(2,128)} %src_hbm.1, s32[1,8]{1,0:T(1,128)} %block_hbm.1, s32[1,8]{1,0:T(1,128)} %live_hbm.1, bf16[2,128,256]{2,1,0:T(8,128)(2,1)} %bitcast.4, bf16[256,256]{1,0:T(8,128)(2,1)} %w_self_hbm.1, ...), custom_call_target="tpu_custom_call" | custom-call | tf_op jit(solution)/shard_map/pallas_call | solution.py:339
  36.2 0.8 %fusion = (f32[256,256]{1,0:T(8,128)}, f32[256,256]{1,0:T(8,128)}) fusion(bf16[512,256]{1,0:T(8,128)(2,1)S(1)} %get-tuple-element.6), kind=kLoop, calls=%fused_computation | loop fusion | bytes 1048576 | tf_op jit(solution)/shard_map/slice | solution.py:397
  37.1 0.7 %copy.14 = bf16[256,256]{1,0:T(8,128)(2,1)} copy(bf16[256,256]{1,0:T(8,128)(2,1)S(1)} %bitcast.3) | data formatting | bytes 262144

commit v5 on v4

--- a/solution.py
+++ b/solution.py
@@ -9,11 +9,12 @@
 
 MESH = pl.DeviceIdType.MESH
 PACK = 16
+FEW = 4
 ORDERS = (("grp", "dom"), ("dom", "grp"))
 
 
 def piece_rows(rows, n):
-    return rows // n if rows % (PACK * n) == 0 else rows
+    return rows // n if n > FEW and rows % (PACK * n) == 0 else rows
 
 
 def f32_dot(a, b):
@@ -100,6 +101,11 @@
             copy.start()
         return copies
 
+    barrier = pltpu.get_barrier_semaphore()
+    for o in range(1, n_dom):
+        pl.semaphore_signal(barrier, inc=1, device_id={"dom": dom_peer[o]}, device_id_type=MESH)
+    for o in range(1, n_grp):
+        pl.semaphore_signal(barrier, inc=1, device_id={"grp": grp_peer[o]}, device_id_type=MESH)
     loads = begin(
         [
             pltpu.make_async_copy(src, dst, load_sem.at[i])
@@ -120,11 +126,6 @@
             )
         ]
     )
-    barrier = pltpu.get_barrier_semaphore()
-    for o in range(1, n_dom):
-        pl.semaphore_signal(barrier, inc=1, device_id={"dom": dom_peer[o]}, device_id_type=MESH)
-    for o in range(1, n_grp):
-        pl.semaphore_signal(barrier, inc=1, device_id={"grp": grp_peer[o]}, device_id_type=MESH)
     for load in loads[:3]:
         load.wait()
 
@@ -264,17 +265,32 @@
                 lambda o: f["mid_low"].at[rows_at(peers[f["two"]][o] * f["piece"], f["piece"])]
                 if f["split"]
                 else f["mid_low"],
-                lambda o: f["sums2"].at[o],
+                lambda o: f["sums2"].at[o if f["split"] else here[f["two"]]],
                 s2_send.at[h],
                 s2_recv.at[h],
             )
         )
-    third = []
+    third, fourth = [], []
+
+    def gather(h, f):
+        rows_of = grad_ref.at[f["mine"], f["columns"]]
+        return to_peers(
+            f["one"], lambda o: rows_of, lambda o: rows_of, s4_send.at[h], s4_recv.at[h]
+        )
+
     for h, f in enumerate(flows):
-        total = f["mid"][f["inner"]]
-        for o, copy in enumerate(second[h], 1):
-            copy.wait_recv()
-            total = total + f["sums2"][o].astype(jnp.float32)
+        if f["split"]:
+            total = f["mid"][f["inner"]]
+            for o, copy in enumerate(second[h], 1):
+                copy.wait_recv()
+                total = total + f["sums2"][o].astype(jnp.float32)
+        else:
+            f["sums2"][here[f["two"]]] = f["mid_low"][...]
+            for copy in second[h]:
+                copy.wait_recv()
+            total = f["sums2"][0].astype(jnp.float32)
+            for o in range(1, count[f["two"]]):
+                total = total + f["sums2"][o].astype(jnp.float32)
         grad_ref[f["spot"], f["columns"]] = total.astype(jnp.bfloat16)
         if f["split"]:
             block_of = grad_ref.at[f["spot"], f["columns"]]
@@ -289,18 +305,12 @@
             )
         else:
             third.append([])
-    fourth = []
+            fourth += gather(h, f)
     for h, f in enumerate(flows):
-        for copy in third[h]:
-            copy.wait_recv()
-        rows_of = grad_ref.at[f["mine"], f["columns"]]
-        fourth += to_peers(
-            f["one"],
-            lambda o: rows_of,
-            lambda o: rows_of,
-            s4_send.at[h],
-            s4_recv.at[h],
-        )
+        if f["split"]:
+            for copy in third[h]:
+                copy.wait_recv()
+            fourth += gather(h, f)
     for copy in fourth:
         copy.wait_recv()
 

time: 37.9 us -> 36.8 us (0.971)
  Pallas kernels: 35.6 us -> 34.5 us
    pallas_call x1, Pallas kernels: 35.6 us -> 34.5 us  [body(): pl.pallas_call(functools.partial(kernel, n_dom, n_grp), out_shape=(jax.Sh...]
where the time goes in v5:
time: 36.8 us; the launch traced here: 36.7 us
  Pallas kernels  34.5 us (94%)
  local copies, waits for them, and re-layouts  1.48 us (4%)
  between operations  0.64 us (2%)
    pallas_call x1, Pallas kernels, body(): pl.pallas_call(functools.partial(kernel, n_dom, n_grp), out_shape=(jax.Sh...  34.5 us
    slice x1, local copies, waits for them, and re-layouts, body(): return (out.reshape(feats.shape), summed[:features], summed[features:])  0.83 us

profile of v5, /device:TPU:0, one launch (start us, length us, event | category | flops | bytes accessed | tf_op | source)
XLA Modules:
  0.0 36.7 jit_solution(13188101349612448119)
XLA Ops:
  0.6 34.5 %shard_map.121 = (bf16[2,128,256]{2,1,0:T(8,128)(2,1)S(1)}, bf16[512,256]{1,0:T(8,128)(2,1)S(1)}) custom-call(s32[2,3]{1,0:T(2,128)} %cols_hbm.1, s32[2,10]{1,0:T(2,128)} %src_hbm.1, s32[1,8]{1,0:T(1,128)} %block_hbm.1, s32[1,8]{1,0:T(1,128)} %live_hbm.1, bf16[2,128,256]{2,1,0:T(8,128)(2,1)} %bitcast.4, bf16[256,256]{1,0:T(8,128)(2,1)} %w_self_hbm.1, ...), custom_call_target="tpu_custom_call" | custom-call | tf_op jit(solution)/shard_map/pallas_call | solution.py:349
  35.2 0.8 %fusion = (f32[256,256]{1,0:T(8,128)}, f32[256,256]{1,0:T(8,128)}) fusion(bf16[512,256]{1,0:T(8,128)(2,1)S(1)} %get-tuple-element.6), kind=kLoop, calls=%fused_computation | loop fusion | bytes 1048576 | tf_op jit(solution)/shard_map/slice | solution.py:407
  36.0 0.7 %copy.14 = bf16[256,256]{1,0:T(8,128)(2,1)} copy(bf16[256,256]{1,0:T(8,128)(2,1)S(1)} %bitcast.3) | data formatting | bytes 262144

commit v6 on v5

--- a/solution.py
+++ b/solution.py
@@ -139,7 +139,7 @@
     far_copies = begin(
         [
             remote(outgoing.at[o], far.at[o], far_send.at[o], far_recv.at[o], o, "dom")
-            for o in range(1, n_dom)
+            for o in sorted(range(1, n_dom), key=lambda o: abs(2 * o - n_dom))
         ]
     )
     near_copies = begin(

time: 36.8 us -> 36.4 us (0.989)
  Pallas kernels: 34.5 us -> 34.1 us
    pallas_call x1, Pallas kernels: 34.5 us -> 34.1 us  [body(): pl.pallas_call(functools.partial(kernel, n_dom, n_grp), out_shape=(jax.Sh...]
where the time goes in v6:
time: 36.4 us; the launch traced here: 36.3 us
  Pallas kernels  34.1 us (94%)
  local copies, waits for them, and re-layouts  1.48 us (4%)
  between operations  0.64 us (2%)
    pallas_call x1, Pallas kernels, body(): pl.pallas_call(functools.partial(kernel, n_dom, n_grp), out_shape=(jax.Sh...  34.1 us
    slice x1, local copies, waits for them, and re-layouts, body(): return (out.reshape(feats.shape), summed[:features], summed[features:])  0.83 us

profile of v6, /device:TPU:0, one launch (start us, length us, event | category | flops | bytes accessed | tf_op | source)
XLA Modules:
  0.0 36.3 jit_solution(12917190124769699333)
XLA Ops:
  0.6 34.1 %shard_map.121 = (bf16[2,128,256]{2,1,0:T(8,128)(2,1)S(1)}, bf16[512,256]{1,0:T(8,128)(2,1)S(1)}) custom-call(s32[2,3]{1,0:T(2,128)} %cols_hbm.1, s32[2,10]{1,0:T(2,128)} %src_hbm.1, s32[1,8]{1,0:T(1,128)} %block_hbm.1, s32[1,8]{1,0:T(1,128)} %live_hbm.1, bf16[2,128,256]{2,1,0:T(8,128)(2,1)} %bitcast.4, bf16[256,256]{1,0:T(8,128)(2,1)} %w_self_hbm.1, ...), custom_call_target="tpu_custom_call" | custom-call | tf_op jit(solution)/shard_map/pallas_call | solution.py:349
  34.8 0.8 %fusion = (f32[256,256]{1,0:T(8,128)}, f32[256,256]{1,0:T(8,128)}) fusion(bf16[512,256]{1,0:T(8,128)(2,1)S(1)} %get-tuple-element.6), kind=kLoop, calls=%fused_computation | loop fusion | bytes 1048576 | tf_op jit(solution)/shard_map/slice | solution.py:407
  35.6 0.7 %copy.14 = bf16[256,256]{1,0:T(8,128)(2,1)} copy(bf16[256,256]{1,0:T(8,128)(2,1)S(1)} %bitcast.3) | data formatting | bytes 262144
